TPU v7x, 256 devices: a whole 4x4x8 slice. The times are simulated.
256 devices in a mesh: chan: 8 (over x, core), ctx: 32 (over z, y).
Axes of the slice: x: 4, y: 4, z: 8, core: 2. Of those that a mesh axis runs over, the one named last changes fastest.
Arguments:
- queries: bfloat16 [4096, 8192], P('ctx', 'chan'), may hold values from -6 to 6
- keys: bfloat16 [4096, 8192], P('ctx', 'chan'), may hold values from -6 to 6
- values: bfloat16 [4096, 8192], P('ctx', 'chan'), may hold values from -6 to 6
- filters: bfloat16 [4, 4096], P(None, 'ctx'), may hold values from -0.09375 to 0.09375
- cotangent: bfloat16 [4096, 8192], P('ctx', 'chan'), may hold values from -6 to 6
Outputs:
- output: bfloat16 [4096, 8192], P('ctx', 'chan')
- query_grad: bfloat16 [4096, 8192], P('ctx', 'chan')
- key_grad: bfloat16 [4096, 8192], P('ctx', 'chan')
- value_grad: bfloat16 [4096, 8192], P('ctx', 'chan')
- filter_grad: float32 [4, 4096], P(None, 'ctx')
All inputs are finite; a program needn't handle non-finite values.
Results may differ from a plain program's by a relative error of at most 0.015.
Values may be sent and summed in bfloat16 or wider, within the bound.
A program may use at most 64 MiB of HBM per device.

v0:
```python
import jax
import jax.numpy as jnp
from jax import lax
from jax.sharding import PartitionSpec as P

D = 8192
NFILT = 4


def toeplitz(padded, base, height, breadth):
    middle = padded.shape[1] // 2
    span = height + breadth - 1
    window = lax.dynamic_slice_in_dim(padded, middle + base - breadth + 1, span, 1)
    flipped = window[:, ::-1]
    tiled = jnp.tile(flipped, (1, height + 1))
    flat = tiled[:, height - 1 : height - 1 + height * (span - 1)]
    return flat.reshape(padded.shape[0], height, span - 1)[:, :, :breadth]


def diagonal_sums(product):
    nfil, height, breadth = product.shape
    stride = height + breadth
    flipped = product[:, :, ::-1]
    padded = jnp.pad(flipped, ((0, 0), (0, 0), (0, height)))
    flat = padded.reshape(nfil, height * stride)[:, : height * (stride - 1)]
    return jnp.sum(flat.reshape(nfil, height, stride - 1), axis=1)


def add_lags(lag_acc, sums, first_lag):
    middle = lag_acc.shape[1] // 2
    where = middle + first_lag
    current = lax.dynamic_slice_in_dim(lag_acc, where, sums.shape[1], 1)
    return lax.dynamic_update_slice_in_dim(lag_acc, current + sums, where, 1)


def in_blocks(block_fn, carry, piece, rows):
    count = piece.shape[0]
    size = rows * max(1, 512 // rows)
    parts = piece.reshape((count // size, size) + piece.shape[1:])
    offsets = jnp.arange(count // size, dtype=jnp.int32) * size

    def visit(state, item):
        block, offset = item
        return (block_fn(state, block, offset), None)

    result, unused = lax.scan(visit, carry, (parts, offsets))
    return result


def shards(queries, keys, values, filters, cotangent):
    rows, width = queries.shape
    nfil = filters.shape[0]
    narrow = width // nfil
    gated = (keys.astype(jnp.float32) * values.astype(jnp.float32)).astype(jnp.bfloat16)
    back = (cotangent.astype(jnp.float32) * queries.astype(jnp.float32)).astype(jnp.bfloat16)
    taps = lax.all_gather(filters, "ctx", axis=1, tiled=True)
    total = taps.shape[1]
    padded = jnp.concatenate([jnp.zeros_like(taps), taps], axis=1)
    lag_start = jnp.zeros((nfil, 2 * total), jnp.float32)
    first = lax.axis_index("ctx") * rows
    back_cols = back.reshape(rows, narrow, nfil)

    def forward_block(carry, piece, start):
        count = piece.shape[0]

        def forward_work(state):
            mixed_acc, lag_acc = state
            tile = toeplitz(padded, first - start, rows, count)
            columns = piece.reshape(count, narrow, nfil)
            mixed_acc = mixed_acc + jnp.einsum(
                "fst,tcf->scf", tile, columns, preferred_element_type=jnp.float32
            )
            product = jnp.einsum(
                "scf,tcf->fst", back_cols, columns, preferred_element_type=jnp.float32
            )
            lag_acc = add_lags(lag_acc, diagonal_sums(product), first - start - count + 1)
            return (mixed_acc, lag_acc)

        return lax.cond(start < first + rows, forward_work, lambda state: state, carry)

    empty = jnp.zeros((rows, narrow, nfil), jnp.float32)
    mixed_acc, lag_part = in_blocks(
        forward_block, (empty, lag_start), lax.all_gather(gated, "ctx", axis=0, tiled=True), rows
    )

    def backward_block(grad_acc, piece, start):
        count = piece.shape[0]

        def backward_work(state):
            tile = toeplitz(padded, start - first, count, rows)
            columns = piece.reshape(count, narrow, nfil)
            return state + jnp.einsum(
                "fst,scf->tcf", tile, columns, preferred_element_type=jnp.float32
            )

        return lax.cond(start + count > first, backward_work, lambda state: state, grad_acc)

    grad_acc = in_blocks(
        backward_block, empty, lax.all_gather(back, "ctx", axis=0, tiled=True), rows
    )
    mixed = mixed_acc.reshape(rows, width)
    gated_grad = grad_acc.reshape(rows, width)
    lag_share = lax.psum_scatter(
        lag_part[:, total:].astype(jnp.bfloat16), "ctx", scatter_dimension=1, tiled=True
    ).astype(jnp.float32)
    lag_total = lax.psum(lag_share, "chan")
    scale = (total * (D // NFILT)) ** (-0.5)
    filter_grad = lag_total * scale
    output = (queries.astype(jnp.float32) * mixed).astype(jnp.bfloat16)
    query_grad = (cotangent.astype(jnp.float32) * mixed).astype(jnp.bfloat16)
    key_grad = (gated_grad * values.astype(jnp.float32)).astype(jnp.bfloat16)
    value_grad = (gated_grad * keys.astype(jnp.float32)).astype(jnp.bfloat16)
    return (output, query_grad, key_grad, value_grad, filter_grad)


def solution(mesh):
    placed = (
        P("ctx", "chan"),
        P("ctx", "chan"),
        P("ctx", "chan"),
        P(None, "ctx"),
        P("ctx", "chan"),
    )
    return jax.shard_map(
        shards,
        mesh=mesh,
        in_specs=placed,
        out_specs=(
            P("ctx", "chan"),
            P("ctx", "chan"),
            P("ctx", "chan"),
            P("ctx", "chan"),
            P(None, "ctx"),
        ),
        check_vma=False,
    )
```

profile of v0, /device:TPU:1, one launch (start us, length us, event | category | flops | bytes accessed | tf_op | source)
XLA Modules:
  0.0 846.8 jit_solution(6806432111096197766)
XLA Ops:
  12.5 38.3 %all_gather.9 = bf16[4,4096]{1,0:T(4,128)(2,1)S(1)} all-gather(bf16[4,128]{1,0:T(4,128)(2,1)S(1)} %copy-done.7), channel_id=1, replica_groups=mesh['chan'=8,'ctx'=32] {'ctx'}, dimensions={1}, use_global_device_ids=true | all-gather | bytes 33792 | tf_op jit(solution)/shard_map/all_gather | solution.py:56
  50.8 65.4 %all-gather.5.cloned.1.call-done = bf16[4096,1024]{0,1:T(8,128)(2,1)} async-done(((bf16[128,1024]{0,1:T(8,128)(2,1)}), bf16[4096,1024]{0,1:T(8,128)(2,1)}) %all-gather.5.cloned.1.call-update) | async-done | bytes 8388624 | tf_op jit(solution)/shard_map/all_gather | solution.py:99
  116.2 7.4 copy.60
  123.7 238.9 %while.27 = (s32[]{:T(128)}, f32[128,256,4]{1,0,2:T(8,128)S(1)}, s32[8]{0:T(128)S(1)}, s32[]{:T(128)}, bf16[4,8192]{1,0:T(4,128)(2,1)S(1)}, /*index=5*/bf16[8,512,1024]{1,2,0:T(8,128)(2,1)}, s32[]{:T(128)}, s32[]{:T(128)}) while((s32[]{:T(128)}, f32[128,256,4]{1,0,2:T(8,128)S(1)}, s32[8]{0:T(128)S(1)}, s32[]{:T(128)}, ...), condition=%wide.region_8.9_spmd, body=%wide.region_5.8_spmd.sunk | while | flops 134348800 | bytes 35643552 | solution.py:46
  125.0 28.5 %conditional.5 = (f32[128,256,4]{1,0,2:T(8,128)S(1)}) conditional(s32[]{:T(128)} %convert_element_type.91, f32[128,256,4]{1,0,2:T(8,128)S(1)} %get-tuple-element.399, (s32[]{:T(128)}, s32[]{:T(128)}, bf16[4,8192]{1,0:T(4,128)(2,1)S(1)}, bf16[8,512,1024]{1,2,0:T(8,128)(2,1)}, s32[]{:T(128)}, /*index=5*/f32[128,256,4]{1,0,2:T(8,128)S(1)}) %tuple.73), branch_computations={%region_6.6_spmd, %region_7.7_spmd} | conditional | flops 134348800 | bytes 35643384 | solution.py:96
  126.6 6.1 reshape.68
  132.7 5.1 tile.14
  137.8 3.0 slice.28
  140.8 2.7 reshape.70
  143.5 6.8 reshape.54
  151.9 1.6 fusion.2
  154.9 28.5 %conditional.5 = (f32[128,256,4]{1,0,2:T(8,128)S(1)}) conditional(s32[]{:T(128)} %convert_element_type.91, f32[128,256,4]{1,0,2:T(8,128)S(1)} %get-tuple-element.399, (s32[]{:T(128)}, s32[]{:T(128)}, bf16[4,8192]{1,0:T(4,128)(2,1)S(1)}, bf16[8,512,1024]{1,2,0:T(8,128)(2,1)}, s32[]{:T(128)}, /*index=5*/f32[128,256,4]{1,0,2:T(8,128)S(1)}) %tuple.73), branch_computations={%region_6.6_spmd, %region_7.7_spmd} | conditional | flops 134348800 | bytes 35643384 | solution.py:96
  156.5 6.1 reshape.68
  162.6 5.1 tile.14
  167.7 3.0 slice.28
  170.7 2.7 reshape.70
  173.4 6.8 reshape.54
  184.8 28.5 %conditional.5 = (f32[128,256,4]{1,0,2:T(8,128)S(1)}) conditional(s32[]{:T(128)} %convert_element_type.91, f32[128,256,4]{1,0,2:T(8,128)S(1)} %get-tuple-element.399, (s32[]{:T(128)}, s32[]{:T(128)}, bf16[4,8192]{1,0:T(4,128)(2,1)S(1)}, bf16[8,512,1024]{1,2,0:T(8,128)(2,1)}, s32[]{:T(128)}, /*index=5*/f32[128,256,4]{1,0,2:T(8,128)S(1)}) %tuple.73), branch_computations={%region_6.6_spmd, %region_7.7_spmd} | conditional | flops 134348800 | bytes 35643384 | solution.py:96
  186.3 6.1 reshape.68
  192.4 5.1 tile.14
  197.5 3.0 slice.28
  200.5 2.7 reshape.70
  203.2 6.8 reshape.54
  214.6 28.5 %conditional.5 = (f32[128,256,4]{1,0,2:T(8,128)S(1)}) conditional(s32[]{:T(128)} %convert_element_type.91, f32[128,256,4]{1,0,2:T(8,128)S(1)} %get-tuple-element.399, (s32[]{:T(128)}, s32[]{:T(128)}, bf16[4,8192]{1,0:T(4,128)(2,1)S(1)}, bf16[8,512,1024]{1,2,0:T(8,128)(2,1)}, s32[]{:T(128)}, /*index=5*/f32[128,256,4]{1,0,2:T(8,128)S(1)}) %tuple.73), branch_computations={%region_6.6_spmd, %region_7.7_spmd} | conditional | flops 134348800 | bytes 35643384 | solution.py:96
  216.2 6.1 reshape.68
  222.3 5.1 tile.14
  227.4 3.0 slice.28
  230.4 2.7 reshape.70
  233.1 6.8 reshape.54
  244.5 28.5 %conditional.5 = (f32[128,256,4]{1,0,2:T(8,128)S(1)}) conditional(s32[]{:T(128)} %convert_element_type.91, f32[128,256,4]{1,0,2:T(8,128)S(1)} %get-tuple-element.399, (s32[]{:T(128)}, s32[]{:T(128)}, bf16[4,8192]{1,0:T(4,128)(2,1)S(1)}, bf16[8,512,1024]{1,2,0:T(8,128)(2,1)}, s32[]{:T(128)}, /*index=5*/f32[128,256,4]{1,0,2:T(8,128)S(1)}) %tuple.73), branch_computations={%region_6.6_spmd, %region_7.7_spmd} | conditional | flops 134348800 | bytes 35643384 | solution.py:96
  246.1 6.1 reshape.68
  252.1 5.1 tile.14
  257.3 3.0 slice.28
  260.2 2.7 reshape.70
  263.0 6.8 reshape.54
  271.4 1.6 fusion.2
  274.4 28.5 %conditional.5 = (f32[128,256,4]{1,0,2:T(8,128)S(1)}) conditional(s32[]{:T(128)} %convert_element_type.91, f32[128,256,4]{1,0,2:T(8,128)S(1)} %get-tuple-element.399, (s32[]{:T(128)}, s32[]{:T(128)}, bf16[4,8192]{1,0:T(4,128)(2,1)S(1)}, bf16[8,512,1024]{1,2,0:T(8,128)(2,1)}, s32[]{:T(128)}, /*index=5*/f32[128,256,4]{1,0,2:T(8,128)S(1)}) %tuple.73), branch_computations={%region_6.6_spmd, %region_7.7_spmd} | conditional | flops 134348800 | bytes 35643384 | solution.py:96
  275.9 6.1 reshape.68
  282.0 5.1 tile.14
  287.1 3.0 slice.28
  290.1 2.7 reshape.70
  292.8 6.8 reshape.54
  304.2 28.5 %conditional.5 = (f32[128,256,4]{1,0,2:T(8,128)S(1)}) conditional(s32[]{:T(128)} %convert_element_type.91, f32[128,256,4]{1,0,2:T(8,128)S(1)} %get-tuple-element.399, (s32[]{:T(128)}, s32[]{:T(128)}, bf16[4,8192]{1,0:T(4,128)(2,1)S(1)}, bf16[8,512,1024]{1,2,0:T(8,128)(2,1)}, s32[]{:T(128)}, /*index=5*/f32[128,256,4]{1,0,2:T(8,128)S(1)}) %tuple.73), branch_computations={%region_6.6_spmd, %region_7.7_spmd} | conditional | flops 134348800 | bytes 35643384 | solution.py:96
  305.8 6.1 reshape.68
  311.9 5.1 tile.14
  317.0 3.0 slice.28
  320.0 2.7 reshape.70
  322.7 6.8 reshape.54
  331.1 1.6 fusion.2
  334.1 28.5 %conditional.5 = (f32[128,256,4]{1,0,2:T(8,128)S(1)}) conditional(s32[]{:T(128)} %convert_element_type.91, f32[128,256,4]{1,0,2:T(8,128)S(1)} %get-tuple-element.399, (s32[]{:T(128)}, s32[]{:T(128)}, bf16[4,8192]{1,0:T(4,128)(2,1)S(1)}, bf16[8,512,1024]{1,2,0:T(8,128)(2,1)}, s32[]{:T(128)}, /*index=5*/f32[128,256,4]{1,0,2:T(8,128)S(1)}) %tuple.73), branch_computations={%region_6.6_spmd, %region_7.7_spmd} | conditional | flops 134348800 | bytes 35643384 | solution.py:96
  335.6 6.1 reshape.68
  341.7 5.1 tile.14
  346.9 3.0 slice.28
  349.8 2.7 reshape.70
  352.6 6.8 reshape.54
  362.9 1.8 fusion.6
  366.8 96.9 %all-gather.3.cloned.1.call-done = bf16[4096,1024]{0,1:T(8,128)(2,1)} async-done(((bf16[128,1024]{0,1:T(8,128)(2,1)}), bf16[4096,1024]{0,1:T(8,128)(2,1)}) %all-gather.3.cloned.1.call-update) | async-done | bytes 8388624 | tf_op jit(solution)/shard_map/all_gather | solution.py:83
  463.7 7.4 copy.61
  471.9 26.2 %while.26 = (s32[]{:T(128)}, f32[128,256,4]{1,0,2:T(8,128)}, f32[4,8192]{1,0:T(4,128)S(1)}, s32[8]{0:T(128)S(1)}, s32[]{:T(128)}, /*index=5*/s32[]{:T(128)}, bf1...) while((s32[]{:T(128)}, f32[128,256,4]{1,0,2:T(8,128)}, ...), condition=%wide.region_4.5_spmd, body=%wide.region_0.4_spmd.sunk | while | flops 268893696 | bytes 31679636 | solution.py:46
  473.2 16.0 %conditional.4 = ((f32[128,256,4]{1,0,2:T(8,128)}, f32[4,8192]{1,0:T(4,128)S(1)})) conditional(s32[]{:T(128)} %convert_element_type.90, (f32[128,256,4]{1,0,2:T(8,128)}, f32[4,8192]{1,0:T(4,128)S(1)}) %tuple.70, (s32[]{:T(128)}, s32[]{:T(128)}, bf16[4,8192]{1,0:T(4,128)(2,1)}, bf16[8,512,1024]{1,2,0:T(8,128)(2,1)}, s32[]{:T(128)}, ...), branch_computations={%region_1.1_spmd, %region_2.3_spmd} | conditional | flops 268893696 | bytes 31679430 | solution.py:79
  479.7 2.9 reshape.53
  487.0 2.1 fusion
  502.8 318.5 %reduce-scatter.4.cloned.1.call-done = bf16[128,4]{1,0:T(8,128)(2,1)} async-done(((bf16[4096,4]{1,0:T(8,128)(2,1)}), bf16[128,4]{1,0:T(8,128)(2,1)}) %reduce-scatter.4.cloned.1.call-update) | async-done | bytes 1040
  822.1 17.6 %psum.7 = f32[4,128]{1,0:T(4,128)S(1)} all-reduce(bf16[4,128]{1,0:T(4,128)(2,1)S(1)} %copy.50), channel_id=1, replica_groups=mesh['chan'=8,'ctx'=32] {'chan'}, use_global_device_ids=true, to_apply=%region_10.11 | all-reduce | flops 512 | bytes 3072 | tf_op jit(solution)/shard_map/psum | solution.py:106
  (139 shorter events, 61.9 us)
Async XLA Ops:
  7.2 4.5 copy-start.5
  7.2 5.3 copy-start.7
  7.2 109.0 %all-gather.5.cloned.1.call-start = ((), (), s32[]{:S(2)}) async-start(), calls=%async_computation.2 | async-start | bytes 8650752 | tf_op jit(solution)/shard_map/all_gather | solution.py:99
  8.4 115.2 %copy-start.1 = (bf16[128,1024]{0,1:T(8,128)(2,1)}, bf16[128,1024]{0,1:T(8,128)(2,1)S(1)}, u32[]{:S(2)}) copy-start(bf16[128,1024]{0,1:T(8,128)(2,1)S(1)} %copy.36) | copy-start | bytes 786436
  9.6 114.0 %copy-start.3 = (bf16[128,1024]{0,1:T(8,128)(2,1)}, bf16[128,1024]{0,1:T(8,128)(2,1)S(1)}, u32[]{:S(2)}) copy-start(bf16[128,1024]{0,1:T(8,128)(2,1)S(1)} %copy.39) | copy-start | bytes 786436
  10.4 453.2 %all-gather.3.cloned.1.call-start = ((), (), s32[]{:S(2)}) async-start(), calls=%async_computation.1 | async-start | bytes 8650752 | tf_op jit(solution)/shard_map/all_gather | solution.py:83
  362.6 108.5 %copy-start.6 = (bf16[4,8192]{1,0:T(4,128)(2,1)}, bf16[4,8192]{1,0:T(4,128)(2,1)S(1)}, u32[]{:S(2)}) copy-start(bf16[4,8192]{1,0:T(4,128)(2,1)S(1)} %get-tuple-element.458) | copy-start | bytes 196612
  362.6 2.3 copy-start
  364.7 456.6 %reduce-scatter.4.cloned.1.call-start = ((), (), s32[]{:S(2)}) async-start(), calls=%async_computation.3 | async-start | bytes 1081344
  498.1 2.8 copy-start.2
  498.1 2.8 copy-start.4
Sparse Core Ops, SparseCore 0:
  11.1 105.0 all-gather.4
  364.8 98.8 all-gather.2
  501.1 320.1 reduce-scatter.3
where the time goes:
time: 849 us; the launch traced here: 847 us
  waiting for transfers between devices  481 us (57%)
  local copies, waits for them, and re-layouts  259 us (31%)
  blocking collectives  56 us (7%)
  loops' own time  17.9 us (2%)
  matrix products  15.2 us (2%)
  between operations  14 us (2%)
    unnamed x4, waiting for transfers between devices  319 us
    all_gather x1, waiting for transfers between devices, shards(): lax.all_gather(gated, 'ctx', axis=0, tiled=True)  96.9 us
    cond x37, local copies, waits for them, and re-layouts  76.6 us
    all_gather x1, waiting for transfers between devices, shards(): lax.all_gather(back, 'ctx', axis=0, tiled=True)  65.4 us
    reshape x9, local copies, waits for them, and re-layouts, toeplitz(): return flat.reshape(padded.shape[0], height, span - 1)[:, :, :breadth]  56.2 us
    another operation x18, local copies, waits for them, and re-layouts, toeplitz(): tiled = jnp.tile(flipped, (1, height + 1))  43.2 us
    all_gather x1, blocking collectives, shards(): taps = lax.all_gather(filters, 'ctx', axis=1, tiled=True)  38.3 us
    slice x9, local copies, waits for them, and re-layouts, toeplitz(): flat = tiled[:, height - 1:height - 1 + height * (span - 1)]  24.4 us
  transfers between devices with their start and end apart: 3, of which 3 were waited for; matrix products, arithmetic and copies ran while one was open for 1% of the time, Pallas kernels for 0%

commit v1 on v0

--- a/solution.py
+++ b/solution.py
@@ -80,7 +80,12 @@
 
     empty = jnp.zeros((rows, narrow, nfil), jnp.float32)
     mixed_acc, lag_part = in_blocks(
-        forward_block, (empty, lag_start), lax.all_gather(gated, "ctx", axis=0, tiled=True), rows
+        forward_block,
+        (empty, lag_start),
+        jnp.concatenate(
+            lax.all_to_all(jnp.stack([gated] * lax.axis_size("ctx")), "ctx", 0, 0), axis=0
+        ),
+        rows,
     )
 
     def backward_block(grad_acc, piece, start):

time: 849 us -> 943 us (1.11)
  waiting for transfers between devices: 481 us -> 564 us
    all_to_all x0 -> x1, waiting for transfers between devices: none -> 178 us  [shards(): lax.all_to_all(jnp.stack([gated] * lax.axis_size('ctx')), 'ctx', 0, 0)]
    all_gather x1 -> x0, waiting for transfers between devices: 96.9 us -> none  [shards(): lax.all_gather(gated, 'ctx', axis=0, tiled=True)]
    while x3 -> x4, local copies, waits for them, and re-layouts: 1.72 us -> 13.2 us  [in_blocks(): result, unused = lax.scan(visit, carry, (parts, offsets))]
    unnamed x4 -> x3, waiting for transfers between devices: 319 us -> 320 us
where the time goes in v1:
time: 943 us; the launch traced here: 941 us
  waiting for transfers between devices  564 us (60%)
  local copies, waits for them, and re-layouts  267 us (28%)
  blocking collectives  56 us (6%)
  loops' own time  16.2 us (2%)
  matrix products  15.2 us (2%)
  between operations  14.3 us (2%)
    unnamed x3, waiting for transfers between devices  320 us
    all_to_all x1, waiting for transfers between devices, shards(): lax.all_to_all(jnp.stack([gated] * lax.axis_size('ctx')), 'ctx', 0, 0)  178 us
    cond x37, local copies, waits for them, and re-layouts  76.5 us
    all_gather x1, waiting for transfers between devices, shards(): lax.all_gather(back, 'ctx', axis=0, tiled=True)  65.4 us
    reshape x9, local copies, waits for them, and re-layouts, toeplitz(): return flat.reshape(padded.shape[0], height, span - 1)[:, :, :breadth]  56.2 us
    another operation x18, local copies, waits for them, and re-layouts, toeplitz(): tiled = jnp.tile(flipped, (1, height + 1))  43.2 us
    all_gather x1, blocking collectives, shards(): taps = lax.all_gather(filters, 'ctx', axis=1, tiled=True)  38.4 us
    slice x9, local copies, waits for them, and re-layouts, toeplitz(): flat = tiled[:, height - 1:height - 1 + height * (span - 1)]  24.5 us
  transfers between devices with their start and end apart: 3, of which 3 were waited for; matrix products, arithmetic and copies ran while one was open for 1% of the time, Pallas kernels for 0%

profile of v1, /device:TPU:1, one launch (start us, length us, event | category | flops | bytes accessed | tf_op | source)
XLA Modules:
  0.0 940.5 jit_solution(18432276304883272966)
XLA Ops:
  12.4 38.4 %all_gather.6 = bf16[4,4096]{1,0:T(4,128)(2,1)S(1)} all-gather(bf16[4,128]{1,0:T(4,128)(2,1)S(1)} %copy-done.7), channel_id=1, replica_groups=mesh['chan'=8,'ctx'=32] {'ctx'}, dimensions={1}, use_global_device_ids=true | all-gather | bytes 33792 | tf_op jit(solution)/shard_map/all_gather | solution.py:56
  50.8 65.4 %all-gather.2.cloned.1.call-done = bf16[4096,1024]{0,1:T(8,128)(2,1)} async-done(((bf16[128,1024]{0,1:T(8,128)(2,1)}), bf16[4096,1024]{0,1:T(8,128)(2,1)}) %all-gather.2.cloned.1.call-update) | async-done | bytes 8388624 | tf_op jit(solution)/shard_map/all_gather | solution.py:104
  116.2 7.4 copy.78
  123.7 237.5 %while.27 = (s32[]{:T(128)}, f32[128,256,4]{1,0,2:T(8,128)S(1)}, s32[8]{0:T(128)S(1)}, s32[]{:T(128)}, bf16[4,8192]{1,0:T(4,128)(2,1)S(1)}, /*index=5*/bf16[8,512,1024]{1,2,0:T(8,128)(2,1)}, s32[]{:T(128)}, s32[]{:T(128)}) while((s32[]{:T(128)}, f32[128,256,4]{1,0,2:T(8,128)S(1)}, s32[8]{0:T(128)S(1)}, s32[]{:T(128)}, ...), condition=%wide.region_8.9_spmd, body=%wide.region_5.8_spmd.sunk | while | flops 134348800 | bytes 35643552 | solution.py:46
  124.9 28.4 %conditional.5 = (f32[128,256,4]{1,0,2:T(8,128)S(1)}) conditional(s32[]{:T(128)} %convert_element_type.91, f32[128,256,4]{1,0,2:T(8,128)S(1)} %get-tuple-element.419, (s32[]{:T(128)}, s32[]{:T(128)}, bf16[4,8192]{1,0:T(4,128)(2,1)S(1)}, bf16[8,512,1024]{1,2,0:T(8,128)(2,1)}, s32[]{:T(128)}, /*index=5*/f32[128,256,4]{1,0,2:T(8,128)S(1)}) %tuple.76), branch_computations={%region_6.6_spmd, %region_7.7_spmd} | conditional | flops 134348800 | bytes 35643384 | solution.py:101
  126.4 6.1 reshape.66
  132.5 5.1 tile.14
  137.6 3.0 slice.28
  140.6 2.7 reshape.68
  143.3 6.8 reshape.54
  154.6 28.4 %conditional.5 = (f32[128,256,4]{1,0,2:T(8,128)S(1)}) conditional(s32[]{:T(128)} %convert_element_type.91, f32[128,256,4]{1,0,2:T(8,128)S(1)} %get-tuple-element.419, (s32[]{:T(128)}, s32[]{:T(128)}, bf16[4,8192]{1,0:T(4,128)(2,1)S(1)}, bf16[8,512,1024]{1,2,0:T(8,128)(2,1)}, s32[]{:T(128)}, /*index=5*/f32[128,256,4]{1,0,2:T(8,128)S(1)}) %tuple.76), branch_computations={%region_6.6_spmd, %region_7.7_spmd} | conditional | flops 134348800 | bytes 35643384 | solution.py:101
  156.1 6.1 reshape.66
  162.1 5.1 tile.14
  167.3 3.0 slice.28
  170.3 2.7 reshape.68
  173.0 6.8 reshape.54
  184.3 28.4 %conditional.5 = (f32[128,256,4]{1,0,2:T(8,128)S(1)}) conditional(s32[]{:T(128)} %convert_element_type.91, f32[128,256,4]{1,0,2:T(8,128)S(1)} %get-tuple-element.419, (s32[]{:T(128)}, s32[]{:T(128)}, bf16[4,8192]{1,0:T(4,128)(2,1)S(1)}, bf16[8,512,1024]{1,2,0:T(8,128)(2,1)}, s32[]{:T(128)}, /*index=5*/f32[128,256,4]{1,0,2:T(8,128)S(1)}) %tuple.76), branch_computations={%region_6.6_spmd, %region_7.7_spmd} | conditional | flops 134348800 | bytes 35643384 | solution.py:101
  185.7 6.1 reshape.66
  191.8 5.1 tile.14
  196.9 3.0 slice.28
  199.9 2.7 reshape.68
  202.6 6.8 reshape.54
  211.1 1.6 fusion.2
  213.9 28.4 %conditional.5 = (f32[128,256,4]{1,0,2:T(8,128)S(1)}) conditional(s32[]{:T(128)} %convert_element_type.91, f32[128,256,4]{1,0,2:T(8,128)S(1)} %get-tuple-element.419, (s32[]{:T(128)}, s32[]{:T(128)}, bf16[4,8192]{1,0:T(4,128)(2,1)S(1)}, bf16[8,512,1024]{1,2,0:T(8,128)(2,1)}, s32[]{:T(128)}, /*index=5*/f32[128,256,4]{1,0,2:T(8,128)S(1)}) %tuple.76), branch_computations={%region_6.6_spmd, %region_7.7_spmd} | conditional | flops 134348800 | bytes 35643384 | solution.py:101
  215.4 6.1 reshape.66
  221.5 5.1 tile.14
  226.6 3.0 slice.28
  229.6 2.7 reshape.68
  232.3 6.8 reshape.54
  243.6 28.4 %conditional.5 = (f32[128,256,4]{1,0,2:T(8,128)S(1)}) conditional(s32[]{:T(128)} %convert_element_type.91, f32[128,256,4]{1,0,2:T(8,128)S(1)} %get-tuple-element.419, (s32[]{:T(128)}, s32[]{:T(128)}, bf16[4,8192]{1,0:T(4,128)(2,1)S(1)}, bf16[8,512,1024]{1,2,0:T(8,128)(2,1)}, s32[]{:T(128)}, /*index=5*/f32[128,256,4]{1,0,2:T(8,128)S(1)}) %tuple.76), branch_computations={%region_6.6_spmd, %region_7.7_spmd} | conditional | flops 134348800 | bytes 35643384 | solution.py:101
  245.1 6.1 reshape.66
  251.1 5.1 tile.14
  256.3 3.0 slice.28
  259.3 2.7 reshape.68
  262.0 6.8 reshape.54
  273.3 28.4 %conditional.5 = (f32[128,256,4]{1,0,2:T(8,128)S(1)}) conditional(s32[]{:T(128)} %convert_element_type.91, f32[128,256,4]{1,0,2:T(8,128)S(1)} %get-tuple-element.419, (s32[]{:T(128)}, s32[]{:T(128)}, bf16[4,8192]{1,0:T(4,128)(2,1)S(1)}, bf16[8,512,1024]{1,2,0:T(8,128)(2,1)}, s32[]{:T(128)}, /*index=5*/f32[128,256,4]{1,0,2:T(8,128)S(1)}) %tuple.76), branch_computations={%region_6.6_spmd, %region_7.7_spmd} | conditional | flops 134348800 | bytes 35643384 | solution.py:101
  274.7 6.1 reshape.66
  280.8 5.1 tile.14
  285.9 3.0 slice.28
  288.9 2.7 reshape.68
  291.6 6.8 reshape.54
  302.9 28.4 %conditional.5 = (f32[128,256,4]{1,0,2:T(8,128)S(1)}) conditional(s32[]{:T(128)} %convert_element_type.91, f32[128,256,4]{1,0,2:T(8,128)S(1)} %get-tuple-element.419, (s32[]{:T(128)}, s32[]{:T(128)}, bf16[4,8192]{1,0:T(4,128)(2,1)S(1)}, bf16[8,512,1024]{1,2,0:T(8,128)(2,1)}, s32[]{:T(128)}, /*index=5*/f32[128,256,4]{1,0,2:T(8,128)S(1)}) %tuple.76), branch_computations={%region_6.6_spmd, %region_7.7_spmd} | conditional | flops 134348800 | bytes 35643384 | solution.py:101
  304.4 6.1 reshape.66
  310.5 5.1 tile.14
  315.6 3.0 slice.28
  318.6 2.7 reshape.68
  321.3 6.8 reshape.54
  329.8 1.6 fusion.2
  332.6 28.4 %conditional.5 = (f32[128,256,4]{1,0,2:T(8,128)S(1)}) conditional(s32[]{:T(128)} %convert_element_type.91, f32[128,256,4]{1,0,2:T(8,128)S(1)} %get-tuple-element.419, (s32[]{:T(128)}, s32[]{:T(128)}, bf16[4,8192]{1,0:T(4,128)(2,1)S(1)}, bf16[8,512,1024]{1,2,0:T(8,128)(2,1)}, s32[]{:T(128)}, /*index=5*/f32[128,256,4]{1,0,2:T(8,128)S(1)}) %tuple.76), branch_computations={%region_6.6_spmd, %region_7.7_spmd} | conditional | flops 134348800 | bytes 35643384 | solution.py:101
  334.1 6.1 reshape.66
  340.1 5.1 tile.14
  345.3 3.0 slice.28
  348.3 2.7 reshape.68
  351.0 6.8 reshape.54
  362.7 4.3 stack.2
  367.0 5.1 all-to-all-start
  374.1 178.1 %all-to-all-done = bf16[32,128,1024]{2,1,0:T(8,128)(2,1)} async-done(((bf16[32,128,1024]{2,1,0:T(8,128)(2,1)}), bf16[32,128,1024]{2,1,0:T(8,128)(2,1)}, u32[]{:S(2)}, u32[]{:S(2)}) %all-to-all-start) | async-done | bytes 8388640 | tf_op jit(solution)/shard_map/all_to_all | solution.py:86
  552.2 11.5 %copy.60 = bf16[8,512,1024]{1,2,0:T(8,128)(2,1)} copy(bf16[8,512,1024]{2,1,0:T(8,128)(2,1)} %bitcast.5) | data formatting | bytes 16777216 | tf_op jit(solution)/shard_map/while | solution.py:46
  564.5 25.1 %while.26 = (s32[]{:T(128)}, f32[128,256,4]{1,0,2:T(8,128)}, f32[4,8192]{1,0:T(4,128)S(1)}, s32[8]{0:T(128)S(1)}, s32[]{:T(128)}, /*index=5*/s32[]{:T(128)}, bf1...) while((s32[]{:T(128)}, f32[128,256,4]{1,0,2:T(8,128)}, ...), condition=%wide.region_4.5_spmd, body=%wide.region_0.4_spmd.sunk | while | flops 268893696 | bytes 31679636 | solution.py:46
  565.6 15.9 %conditional.4 = ((f32[128,256,4]{1,0,2:T(8,128)}, f32[4,8192]{1,0:T(4,128)S(1)})) conditional(s32[]{:T(128)} %convert_element_type.90, (f32[128,256,4]{1,0,2:T(8,128)}, f32[4,8192]{1,0:T(4,128)S(1)}) %tuple.73, (s32[]{:T(128)}, s32[]{:T(128)}, bf16[4,8192]{1,0:T(4,128)(2,1)}, bf16[8,512,1024]{1,2,0:T(8,128)(2,1)}, s32[]{:T(128)}, ...), branch_computations={%region_1.1_spmd, %region_2.3_spmd} | conditional | flops 268893696 | bytes 31679430 | solution.py:79
  572.0 2.9 reshape.53
  579.4 2.2 fusion
  594.2 320.4 %reduce-scatter.4.cloned.1.call-done = bf16[128,4]{1,0:T(8,128)(2,1)} async-done(((bf16[4096,4]{1,0:T(8,128)(2,1)}), bf16[128,4]{1,0:T(8,128)(2,1)}) %reduce-scatter.4.cloned.1.call-update) | async-done | bytes 1040
  915.4 17.7 %psum.7 = f32[4,128]{1,0:T(4,128)S(1)} all-reduce(bf16[4,128]{1,0:T(4,128)(2,1)S(1)} %copy.70), channel_id=1, replica_groups=mesh['chan'=8,'ctx'=32] {'chan'}, use_global_device_ids=true, to_apply=%region_10.11 | all-reduce | flops 512 | bytes 3072 | tf_op jit(solution)/shard_map/psum | solution.py:111
  (140 shorter events, 63.7 us)
Async XLA Ops:
  7.2 4.4 copy-start.5
  7.2 5.2 copy-start.7
  7.2 109.0 %all-gather.2.cloned.1.call-start = ((), (), s32[]{:S(2)}) async-start(), calls=%async_computation.2 | async-start | bytes 8650752 | tf_op jit(solution)/shard_map/all_gather | solution.py:104
  8.4 115.2 %copy-start.1 = (bf16[128,1024]{0,1:T(8,128)(2,1)}, bf16[128,1024]{0,1:T(8,128)(2,1)S(1)}, u32[]{:S(2)}) copy-start(bf16[128,1024]{0,1:T(8,128)(2,1)S(1)} %copy.55) | copy-start | bytes 786436
  9.6 114.0 %copy-start.3 = (bf16[128,1024]{0,1:T(8,128)(2,1)}, bf16[128,1024]{0,1:T(8,128)(2,1)S(1)}, u32[]{:S(2)}) copy-start(bf16[128,1024]{0,1:T(8,128)(2,1)S(1)} %copy.59) | copy-start | bytes 786436
  361.2 5.8 copy-start.6
  367.0 5.2 copy-start
  367.0 185.2 %all-to-all-start = ((bf16[32,128,1024]{2,1,0:T(8,128)(2,1)}), bf16[32,128,1024]{2,1,0:T(8,128)(2,1)}, u32[]{:S(2)}, u32[]{:S(2)}) async-start(bf16[32,128,1024]{2,1,0:T(8,128)(2,1)} %stack.2), calls=%async_computation | async-start | bytes 16777216 | tf_op jit(solution)/shard_map/all_to_all | solution.py:86
  372.1 542.5 %reduce-scatter.4.cloned.1.call-start = ((), (), s32[]{:S(2)}) async-start(), calls=%async_computation.3 | async-start | bytes 1081344
  589.6 2.8 copy-start.2
  589.6 2.8 copy-start.4
Sparse Core Ops, SparseCore 0:
  11.1 105.1 all-gather.1
  592.5 322.0 reduce-scatter.3
